TPU v7x, 128 devices: a whole 4x4x4 slice. The times are simulated.
128 devices in a mesh: fsdp: 32 (over y, z, core), dp: 4 (over x).
Axes of the slice: x: 4, y: 4, z: 4, core: 2. Of those that a mesh axis runs over, the one named last changes fastest.
Arguments:
- tokens: bfloat16 [16384, 4096], P(('fsdp', 'dp')), may hold values from -6 to 6
- gain: float32 [4096], replicated, may hold values from 0.5 to 1.5
- tiles: bfloat16 [512, 128, 128], P('fsdp'), may hold values from -0.25 to 0.25
- tile_rows: int32 [512], replicated, may hold values from 0 to 31, as said below
- tile_cols: int32 [512], replicated, may hold values from 0 to 111, as said below
- cotangent: bfloat16 [16384, 14336], P(('fsdp', 'dp')), may hold values from -6 to 6
Outputs:
- projected: bfloat16 [16384, 14336], P(('fsdp', 'dp'))
- token_grad: bfloat16 [16384, 4096], P(('fsdp', 'dp'))
- tile_grad: float32 [512, 128, 128], P('fsdp')
- gain_grad: float32 [4096], replicated
Inputs may be any that keep to these rules, and one draw needn't show every extreme that they name: The pairs (tile_rows[i], tile_cols[i]) are all different. `tile_cols`: pairs with tile_rows as above.
All inputs are finite; a program needn't handle non-finite values.
Results may differ from a plain program's by a relative error of at most 0.0049.
Values may be sent and summed in bfloat16 or wider, within the bound.
No kernel may reach another device: no remote copies, remote signals or barrier semaphores. Data moves between devices by JAX's collectives and lax.ppermute only.
A program may use at most 256 MiB of HBM per device.

v0:
```python
import jax
import jax.numpy as jnp
from jax import lax
from jax.sharding import PartitionSpec as P


def shards(tokens, gain, tiles, tile_rows, tile_cols, cotangent):
    count = tokens.shape[0]
    width = tokens.shape[1]
    tile = tiles.shape[1]
    row_blocks = width // tile
    col_blocks = cotangent.shape[1] // tile
    x32 = tokens.astype(jnp.float32)
    scale = lax.rsqrt(jnp.mean(x32 * x32, axis=-1, keepdims=True) + 1e-05)
    normed = (x32 * scale * gain).astype(jnp.bfloat16)
    xblocks = normed.reshape(count, row_blocks, tile)
    gblocks = cotangent.reshape(count, col_blocks, tile)
    piece = lax.all_gather(tiles, "fsdp", axis=0, tiled=True)
    rows = tile_rows
    cols = tile_cols
    xsel = jnp.take(xblocks, rows, axis=1)
    gsel = jnp.take(gblocks, cols, axis=1)
    forward = jnp.einsum("tkj,kjm->tkm", xsel, piece, preferred_element_type=jnp.float32)
    backward = jnp.einsum("tkm,kjm->tkj", gsel, piece, preferred_element_type=jnp.float32)
    stacked = jnp.stack([forward, backward], axis=0)
    outsum = jnp.zeros((count, col_blocks, tile), jnp.float32).at[:, tile_cols].add(stacked[0])
    back = jnp.zeros((count, row_blocks, tile), jnp.float32).at[:, tile_rows].add(stacked[1])
    projected = outsum.reshape(count, col_blocks * tile).astype(jnp.bfloat16)
    dnormed = back.reshape(count, width)
    gain_grad = lax.psum(jnp.sum(dnormed * x32 * scale, axis=0), ("fsdp", "dp"))
    inner = jnp.mean(x32 * gain * dnormed, axis=-1, keepdims=True)
    token_grad = (scale * gain * dnormed - x32 * scale**3 * inner).astype(jnp.bfloat16)
    group = tiles.shape[0]
    number = tiles.shape[0] * lax.axis_size("fsdp")

    def group_terms(first):
        rows = lax.dynamic_slice_in_dim(tile_rows, first, group, 0)
        cols = lax.dynamic_slice_in_dim(tile_cols, first, group, 0)
        xsel = jnp.take(xblocks, rows, axis=1)
        gsel = jnp.take(gblocks, cols, axis=1)
        return jnp.einsum("tkj,tkm->kjm", xsel, gsel, preferred_element_type=jnp.float32)

    firsts = group * jnp.arange(number // group, dtype=jnp.int32)
    result = lax.map(group_terms, firsts)
    owned = lax.psum_scatter(
        result.reshape(number, tile, tile), "fsdp", scatter_dimension=0, tiled=True
    )
    tile_grad = lax.psum(owned, "dp")
    return (projected, token_grad, tile_grad, gain_grad)


def solution(mesh):
    placed = (
        P(("fsdp", "dp"), None),
        P(),
        P("fsdp", None, None),
        P(),
        P(),
        P(("fsdp", "dp"), None),
    )
    return jax.shard_map(
        shards,
        mesh=mesh,
        in_specs=placed,
        out_specs=(P(("fsdp", "dp"), None), P(("fsdp", "dp"), None), P("fsdp", None, None), P()),
        check_vma=False,
    )
```

profile of v0, /device:TPU:1, one launch (start us, length us, event | category | flops | bytes accessed | tf_op | source)
XLA Modules:
  0.0 814.4 jit_solution(1176212291491571832)
XLA Ops:
  8.0 6.1 copy.35
  14.0 6.0 copy.36
  21.7 16.2 %gather_fusion.3 = bf16[512,128,128]{2,1,0:T(8,128)(2,1)} fusion(bf16[128,112,128]{2,0,1:T(8,128)(2,1)} %copy.36, s32[1024]{0:T(1024)S(1)} %pad_clamp_fusion.2), kind=kCustom, calls=%fused_computation.3 | custom fusion | bytes 33556480 | tf_op jit(solution)/shard_map/jit(_take)/gather | solution.py:22
  38.5 48.0 %all-gather.2.cloned.1.call-done = bf16[512,128,128]{2,1,0:T(8,128)(2,1)} async-done(((bf16[16,128,128]{2,1,0:T(8,128)(2,1)}), bf16[512,128,128]{2,1,0:T(8,128)(2,1)}) %all-gather.2.cloned.1.call-update) | async-done | bytes 16777232 | tf_op jit(solution)/shard_map/all_gather | solution.py:18
  86.5 28.2 %fusion.9 = f32[512,128,128]{2,1,0:T(8,128)} fusion(bf16[512,128,128]{2,1,0:T(8,128)(2,1)} %all-gather.2.cloned.1.call-done, bf16[512,128,128]{2,1,0:T(8,128)(2,1)} %gather_fusion.3, pred[512]{0:T(512)(128)(4,1)S(1)} %compare_and_fusion.2), kind=kOutput, calls=%fused_computation.22 | convolution fusion | flops 2155872256 | bytes 67109376 | tf_op jit(solution)/shard_map/tkm,kjm->tkj/dot_general | solution.py:24
  115.0 66.1 %scatter_fusion.1 = f32[128,32,128]{2,0,1:T(8,128)S(1)} fusion(f32[128,32,128]{2,0,1:T(8,128)S(1)} %broadcast_in_dim.69, s32[512]{0:T(512)S(1)} %compare_select_fusion.2, f32[512,128,128]{2,1,0:T(8,128)} %fusion.9), kind=kCustom, calls=%fused_computation.5 | custom fusion | flops 8388608 | bytes 100665344 | tf_op jit(solution)/shard_map/scatter-add | solution.py:27
  185.5 2.8 fusion.24
  189.0 237.1 %while.10 = (s32[]{:T(128)}, f32[32,16,128,128]{3,2,1,0:T(8,128)}, s32[32]{0:T(128)S(1)}, s32[512]{0:T(512)S(1)}, bf16[128,32,128]{2,0,1:T(8,128)(2,1)S(1)}, /*i...) while((s32[]{:T(128)}, f32[32,16,128,128]{3,2,1,0:T(8,128)}, ...), condition=%wide.region_5.6_spmd, body=%wide.region_4.5_spmd.sunk | while | flops 67635392 | bytes 4203735 | solution.py:44
  199.0 2.7 gather_fusion
  213.9 2.7 gather_fusion
  228.7 2.7 gather_fusion
  250.9 2.7 gather_fusion
  317.6 2.7 gather_fusion
  325.0 2.7 gather_fusion
  347.2 2.7 gather_fusion
  426.4 15.0 %gather_fusion.2 = bf16[512,128,128]{2,1,0:T(8,128)(2,1)} fusion(bf16[128,32,128]{2,0,1:T(8,128)(2,1)S(1)} %get-tuple-element.182, s32[1024]{0:T(1024)S(1)} %pad_clamp_fusion.3), kind=kCustom, calls=%fused_computation.2 | custom fusion | bytes 33556480 | tf_op jit(solution)/shard_map/jit(_take)/gather | solution.py:21
  441.3 148.6 %reduce-scatter.2.cloned.1.call-done = f32[16,128,128]{2,1,0:T(8,128)} async-done(((f32[512,128,128]{2,1,0:T(8,128)}), f32[16,128,128]{2,1,0:T(8,128)}) %reduce-scatter.2.cloned.1.call-update) | async-done | bytes 1048592 | tf_op jit(solution)/shard_map/reduce_scatter | solution.py:45
  590.0 24.5 %fusion.11 = f32[512,128,128]{2,1,0:T(8,128)} fusion(bf16[512,128,128]{2,1,0:T(8,128)(2,1)} %all-gather.2.cloned.1.call-done, bf16[512,128,128]{2,1,0:T(8,128)(2,1)} %gather_fusion.2, pred[512]{0:T(512)(128)(4,1)S(1)} %compare_and_fusion.3), kind=kOutput, calls=%fused_computation.24 | convolution fusion | flops 2155872256 | bytes 67109376 | tf_op jit(solution)/shard_map/tkj,kjm->tkm/dot_general | solution.py:23
  614.5 3.8 broadcast_in_dim.64
  618.3 103.4 %scatter_fusion = f32[128,112,128]{2,0,1:T(8,128)} fusion(f32[128,112,128]{2,0,1:T(8,128)} %broadcast_in_dim.64, s32[512]{0:T(512)S(1)} %compare_select_fusion.3, f32[512,128,128]{2,1,0:T(8,128)} %fusion.11), kind=kCustom, calls=%fused_computation.4 | custom fusion | flops 8388608 | bytes 100665344 | tf_op jit(solution)/shard_map/scatter-add | solution.py:26
  721.7 5.8 convert_element_type.17
  727.5 6.1 copy.34
  733.6 6.1 copy.40
  741.0 64.6 %psum.15 = f32[4096]{0:T(1024)} all-reduce(f32[4096]{0:T(1024)S(1)} %get-tuple-element.68), channel_id=1, replica_groups=mesh['fsdp'=32,'dp'=4] {'fsdp','dp'}, use_global_device_ids=true, to_apply=%region_9.10 | all-reduce | flops 4096 | bytes 32768 | tf_op jit(solution)/shard_map/psum | solution.py:30
  (250 shorter events, 167.2 us)
Async XLA Ops:
  7.2 14.5 %copy-start.2 = (s32[512]{0:T(512)S(1)}, s32[512]{0:T(512)}, u32[]{:S(2)}) copy-start(s32[512]{0:T(512)} %param.12) | copy-start | bytes 6148
  7.2 79.4 %all-gather.2.cloned.1.call-start = ((), (), s32[]{:S(2)}) async-start(), calls=%async_computation.1 | async-start | bytes 17301504 | tf_op jit(solution)/shard_map/all_gather | solution.py:18
  7.9 582.1 %reduce-scatter.2.cloned.1.call-start = ((), (), s32[]{:S(2)}) async-start(), calls=%async_computation.2 | async-start | bytes 34603008 | tf_op jit(solution)/shard_map/reduce_scatter | solution.py:45
  21.7 16.8 %copy-start.3 = (s32[512]{0:T(512)S(1)}, s32[512]{0:T(512)}, u32[]{:S(2)}) copy-start(s32[512]{0:T(512)} %param.11) | copy-start | bytes 6148
  115.0 68.0 %copy-start.1 = (f32[4096]{0:T(1024)S(1)}, f32[4096]{0:T(1024)}, u32[]{:S(2)}) copy-start(f32[4096]{0:T(1024)} %param.9) | copy-start | bytes 49156
  426.1 379.5 %all-reduce.2.cloned.1.call-start = ((), (), s32[]{:S(2)}) async-start(), calls=%async_computation.3 | async-start | bytes 2097152 | tf_op jit(solution)/shard_map/psum | solution.py:48
  721.7 18.0 %copy-start = (bf16[128,4096]{0,1:T(8,128)(2,1)S(1)}, bf16[128,4096]{0,1:T(8,128)(2,1)}, u32[]{:S(2)}) copy-start(bf16[128,4096]{0,1:T(8,128)(2,1)} %get-tuple-element.90) | copy-start | bytes 3145732
Sparse Core Ops, SparseCore 0:
  10.3 76.2 all-gather.1
  426.2 163.6 reduce-scatter.1
  592.5 44.0 all-reduce.1
where the time goes:
time: 820 us; the launch traced here: 814 us
  waiting for transfers between devices  197 us (24%)
  local copies, waits for them, and re-layouts  192 us (23%)
  other arithmetic  184 us (22%)
  matrix products  98.3 us (12%)
  blocking collectives  64.6 us (8%)
  loops' own time  63.1 us (8%)
  between operations  13.9 us (2%)
    reduce_scatter x1, waiting for transfers between devices, shards(): lax.psum_scatter(result.reshape(number, tile, tile), 'fsdp', scatter_dime...  149 us
    scatter-add x1, other arithmetic, shards(): jnp.zeros((count, col_blocks, tile), jnp.float32).at[:, tile_cols]  103 us
    gather x32, local copies, waits for them, and re-layouts, group_terms(): gsel = jnp.take(gblocks, cols, axis=1)  85.9 us
    scatter-add x1, other arithmetic, shards(): jnp.zeros((count, row_blocks, tile), jnp.float32).at[:, tile_rows]  66.1 us
    psum x1, blocking collectives, shards(): gain_grad = lax.psum(jnp.sum(dnormed * x32 * scale, axis=0), ('fsdp', 'dp'))  64.6 us
    another operation x1, loops' own time, shards(): result = lax.map(group_terms, firsts)  63.1 us
    all_gather x1, waiting for transfers between devices, shards(): piece = lax.all_gather(tiles, 'fsdp', axis=0, tiled=True)  48 us
    dot_general x32, matrix products, group_terms(): jnp.einsum('tkj,tkm->kjm', xsel, gsel, preferred_element_type=jnp.float32)  45.6 us
  transfers between devices with their start and end apart: 3, of which 2 were waited for; matrix products, arithmetic and copies ran while one was open for 24% of the time, Pallas kernels for 0%

commit v1 on v0

--- a/solution.py
+++ b/solution.py
@@ -15,7 +15,9 @@
     normed = (x32 * scale * gain).astype(jnp.bfloat16)
     xblocks = normed.reshape(count, row_blocks, tile)
     gblocks = cotangent.reshape(count, col_blocks, tile)
-    piece = lax.all_gather(tiles, "fsdp", axis=0, tiled=True)
+    piece = jnp.concatenate(
+        lax.all_to_all(jnp.stack([tiles] * lax.axis_size("fsdp")), "fsdp", 0, 0), axis=0
+    )
     rows = tile_rows
     cols = tile_cols
     xsel = jnp.take(xblocks, rows, axis=1)

time: 820 us -> 1030 us (1.26)
  waiting for transfers between devices: 197 us -> 390 us
    all_to_all x0 -> x1, waiting for transfers between devices: none -> 202 us  [shards(): lax.all_to_all(jnp.stack([tiles] * lax.axis_size('fsdp')), 'fsdp', 0, 0)]
    all_gather x1 -> x0, waiting for transfers between devices: 48 us -> none  [shards(): piece = lax.all_gather(tiles, 'fsdp', axis=0, tiled=True)]
    reduce_scatter x1, waiting for transfers between devices: 149 us -> 189 us  [shards(): lax.psum_scatter(result.reshape(number, tile, tile), 'fsdp', scatter_dime...]
  transfers between devices with their start and end apart: 3 -> 3, of which waited for: 2 -> 2; matrix products, arithmetic and copies ran while one was open for 24% -> 19% of each run, Pallas kernels for 0% -> 0%
where the time goes in v1:
time: 1030 us; the launch traced here: 1020 us
  waiting for transfers between devices  390 us (38%)
  local copies, waits for them, and re-layouts  197 us (19%)
  other arithmetic  183 us (18%)
  matrix products  98.3 us (10%)
  blocking collectives  64.8 us (6%)
  loops' own time  63.1 us (6%)
  between operations  14.2 us (1%)
    all_to_all x1, waiting for transfers between devices, shards(): lax.all_to_all(jnp.stack([tiles] * lax.axis_size('fsdp')), 'fsdp', 0, 0)  202 us
    reduce_scatter x1, waiting for transfers between devices, shards(): lax.psum_scatter(result.reshape(number, tile, tile), 'fsdp', scatter_dime...  189 us
    scatter-add x1, other arithmetic, shards(): jnp.zeros((count, col_blocks, tile), jnp.float32).at[:, tile_cols]  103 us
    gather x32, local copies, waits for them, and re-layouts, group_terms(): gsel = jnp.take(gblocks, cols, axis=1)  85.9 us
    scatter-add x1, other arithmetic, shards(): jnp.zeros((count, row_blocks, tile), jnp.float32).at[:, tile_rows]  66.1 us
    psum x1, blocking collectives, shards(): gain_grad = lax.psum(jnp.sum(dnormed * x32 * scale, axis=0), ('fsdp', 'dp'))  64.8 us
    another operation x1, loops' own time, shards(): result = lax.map(group_terms, firsts)  63.1 us
    dot_general x32, matrix products, group_terms(): jnp.einsum('tkj,tkm->kjm', xsel, gsel, preferred_element_type=jnp.float32)  45.6 us
  transfers between devices with their start and end apart: 3, of which 2 were waited for; matrix products, arithmetic and copies ran while one was open for 19% of the time, Pallas kernels for 0%

profile of v1, /device:TPU:1, one launch (start us, length us, event | category | flops | bytes accessed | tf_op | source)
XLA Modules:
  0.0 1021.6 jit_solution(15683776111831162135)
XLA Ops:
  7.2 7.0 stack.2
  14.2 9.8 all-to-all-start
  24.1 6.1 copy.24
  30.1 6.0 copy.25
  36.9 16.0 %gather_fusion.3 = bf16[512,128,128]{2,1,0:T(8,128)(2,1)} fusion(bf16[128,112,128]{2,0,1:T(8,128)(2,1)} %copy.25, s32[1024]{0:T(1024)S(1)} %pad_clamp_fusion.2), kind=kCustom, calls=%fused_computation.3 | custom fusion | bytes 33556480 | tf_op jit(solution)/shard_map/jit(_take)/gather | solution.py:24
  53.5 201.7 %all-to-all-done = bf16[32,16,128,128]{3,2,1,0:T(8,128)(2,1)} async-done(((bf16[32,16,128,128]{3,2,1,0:T(8,128)(2,1)}), bf16[32,16,128,128]{3,2,1,0:T(8,128)(2,1)}, u32[]{:S(2)}, u32[]{:S(2)}) %all-to-all-start) | async-done | bytes 16777248 | tf_op jit(solution)/shard_map/all_to_all | solution.py:19
  255.2 28.2 %fusion.9 = f32[512,128,128]{2,1,0:T(8,128)} fusion(bf16[512,128,128]{2,1,0:T(8,128)(2,1)} %bitcast.6, bf16[512,128,128]{2,1,0:T(8,128)(2,1)} %gather_fusion.3, pred[512]{0:T(512)(128)(4,1)S(1)} %compare_and_fusion.2), kind=kOutput, calls=%fused_computation.22 | convolution fusion | flops 2155872256 | bytes 67109376 | tf_op jit(solution)/shard_map/tkm,kjm->tkj/dot_general | solution.py:26
  283.6 66.1 %scatter_fusion.1 = f32[128,32,128]{2,0,1:T(8,128)S(1)} fusion(f32[128,32,128]{2,0,1:T(8,128)S(1)} %broadcast_in_dim.69, s32[512]{0:T(512)S(1)} %compare_select_fusion.2, f32[512,128,128]{2,1,0:T(8,128)} %fusion.9), kind=kCustom, calls=%fused_computation.5 | custom fusion | flops 8388608 | bytes 100665344 | tf_op jit(solution)/shard_map/scatter-add | solution.py:29
  356.9 237.1 %while.10 = (s32[]{:T(128)}, f32[32,16,128,128]{3,2,1,0:T(8,128)}, s32[32]{0:T(128)S(1)}, s32[512]{0:T(512)S(1)}, bf16[128,32,128]{2,0,1:T(8,128)(2,1)S(1)}, /*i...) while((s32[]{:T(128)}, f32[32,16,128,128]{3,2,1,0:T(8,128)}, ...), condition=%wide.region_5.6_spmd, body=%wide.region_4.5_spmd.sunk | while | flops 67635392 | bytes 4203735 | solution.py:46
  366.9 2.7 gather_fusion
  374.3 2.7 gather_fusion
  381.7 2.7 gather_fusion
  389.1 2.7 gather_fusion
  396.5 2.7 gather_fusion
  411.4 2.7 gather_fusion
  594.3 13.9 %gather_fusion.2 = bf16[512,128,128]{2,1,0:T(8,128)(2,1)} fusion(bf16[128,32,128]{2,0,1:T(8,128)(2,1)S(1)} %get-tuple-element.170, s32[1024]{0:T(1024)S(1)} %pad_clamp_fusion.3), kind=kCustom, calls=%fused_computation.2 | custom fusion | bytes 33556480 | tf_op jit(solution)/shard_map/jit(_take)/gather | solution.py:23
  608.1 188.6 %reduce-scatter.2.cloned.1.call-done = f32[16,128,128]{2,1,0:T(8,128)} async-done(((f32[512,128,128]{2,1,0:T(8,128)}), f32[16,128,128]{2,1,0:T(8,128)}) %reduce-scatter.2.cloned.1.call-update) | async-done | bytes 1048592 | tf_op jit(solution)/shard_map/reduce_scatter | solution.py:47
  796.7 24.5 %fusion.11 = f32[512,128,128]{2,1,0:T(8,128)} fusion(bf16[512,128,128]{2,1,0:T(8,128)(2,1)} %bitcast.6, bf16[512,128,128]{2,1,0:T(8,128)(2,1)} %gather_fusion.2, pred[512]{0:T(512)(128)(4,1)S(1)} %compare_and_fusion.3), kind=kOutput, calls=%fused_computation.24 | convolution fusion | flops 2155872256 | bytes 67109376 | tf_op jit(solution)/shard_map/tkj,kjm->tkm/dot_general | solution.py:25
  821.2 3.8 broadcast_in_dim.64
  825.1 103.4 %scatter_fusion = f32[128,112,128]{2,0,1:T(8,128)} fusion(f32[128,112,128]{2,0,1:T(8,128)} %broadcast_in_dim.64, s32[512]{0:T(512)S(1)} %compare_select_fusion.3, f32[512,128,128]{2,1,0:T(8,128)} %fusion.11), kind=kCustom, calls=%fused_computation.4 | custom fusion | flops 8388608 | bytes 100665344 | tf_op jit(solution)/shard_map/scatter-add | solution.py:28
  928.4 5.8 convert_element_type.17
  934.2 6.1 copy.23
  940.2 6.1 copy.29
  947.6 64.8 %psum.15 = f32[4096]{0:T(1024)} all-reduce(f32[4096]{0:T(1024)S(1)} %get-tuple-element.57), channel_id=1, replica_groups=mesh['fsdp'=32,'dp'=4] {'fsdp','dp'}, use_global_device_ids=true, to_apply=%region_9.10 | all-reduce | flops 4096 | bytes 32768 | tf_op jit(solution)/shard_map/psum | solution.py:32
  (250 shorter events, 170.3 us)
Async XLA Ops:
  14.2 22.0 %copy-start = (bf16[128,4096]{1,0:T(8,128)(2,1)S(1)}, bf16[128,4096]{1,0:T(8,128)(2,1)}, u32[]{:S(2)}) copy-start(bf16[128,4096]{1,0:T(8,128)(2,1)} %param.8) | copy-start | bytes 3145732
  14.2 241.0 %all-to-all-start = ((bf16[32,16,128,128]{3,2,1,0:T(8,128)(2,1)}), bf16[32,16,128,128]{3,2,1,0:T(8,128)(2,1)}, u32[]{:S(2)}, u32[]{:S(2)}) async-start(bf16[32,16,128,128]{3,2,1,0:T(8,128)(2,1)} %stack.2), calls=%async_computation | async-start | bytes 33554432 | tf_op jit(solution)/shard_map/all_to_all | solution.py:19
  24.0 12.8 %copy-start.2 = (s32[512]{0:T(512)S(1)}, s32[512]{0:T(512)}, u32[]{:S(2)}) copy-start(s32[512]{0:T(512)} %param.12) | copy-start | bytes 6148
  24.0 772.7 %reduce-scatter.2.cloned.1.call-start = ((), (), s32[]{:S(2)}) async-start(), calls=%async_computation.2 | async-start | bytes 34603008 | tf_op jit(solution)/shard_map/reduce_scatter | solution.py:47
  36.8 16.6 %copy-start.3 = (s32[512]{0:T(512)S(1)}, s32[512]{0:T(512)}, u32[]{:S(2)}) copy-start(s32[512]{0:T(512)} %param.11) | copy-start | bytes 6148
  283.6 68.0 %copy-start.1 = (f32[4096]{0:T(1024)S(1)}, f32[4096]{0:T(1024)}, u32[]{:S(2)}) copy-start(f32[4096]{0:T(1024)} %param.9) | copy-start | bytes 49156
  594.0 418.4 %all-reduce.2.cloned.1.call-start = ((), (), s32[]{:S(2)}) async-start(), calls=%async_computation.3 | async-start | bytes 2097152 | tf_op jit(solution)/shard_map/psum | solution.py:50
Sparse Core Ops, SparseCore 0:
  594.1 202.5 reduce-scatter.1
  799.2 44.2 all-reduce.1
